TPU v7x, 512 devices: a whole 4x4x16 slice. The times are simulated.
512 devices in a mesh: section: 2 (over core), dp: 16 (over z), mp: 16 (over y, x).
Axes of the slice: x: 4, y: 4, z: 16, core: 2. Of those that a mesh axis runs over, the one named last changes fastest.
Arguments:
- events: bfloat16 [512, 1024, 512], P(('section', 'dp', 'mp')), may hold values from -6 to 6
- hist_len: int32 [512], P(('section', 'dp', 'mp')), may hold values from 256 to 1024, as said below
- sess_len: int32 [512, 32], P(('section', 'dp', 'mp')), may hold values from 1 to 64, 1024 in all within a row
- w_uvqk: bfloat16 [512, 2048], P('dp'), may hold values from -0.25 to 0.25
- w_out: bfloat16 [512, 512], P('dp'), may hold values from -0.25 to 0.25
- attn_gain: float32 [512], replicated, may hold values from 0.1 to 1.9
- w_in: bfloat16 [512, 4096], P(None, ('section', 'mp')), may hold values from -2 to 2
- ffn_gain: bfloat16 [1, 4096], P(None, ('section', 'mp')), may hold values from 0.099609375 to 1.8984375
- w_up: bfloat16 [4096, 8192], P('section', 'mp'), may hold values from -0.09375 to 0.09375
- w_down: bfloat16 [8192, 4096], P('mp', 'section'), may hold values from -0.0625 to 0.0625
Outputs:
- pooled: bfloat16 [16384, 512], P(('section', 'dp', 'mp'))
- cross_out: bfloat16 [4096, 4096], P(('section', 'dp', 'mp'))
Inputs may be any that keep to these rules, and one draw needn't show every extreme that they name: `hist_len`: some user has all 1024 events valid. `sess_len`: a user's 32 sessions cover all 1024 positions; some session has exactly 64 events.
All inputs are finite; a program needn't handle non-finite values.
Results may differ from a plain program's by a relative error of at most 0.015.
Values may be sent and summed in bfloat16 or wider, within the bound.
A program may use at most 64 MiB of HBM per device.

v0:
```python
import jax
import jax.numpy as jnp
from jax import lax
from jax.sharding import PartitionSpec as P

HEADS = 4
DM = 4096
MICRO = 4


EPSILON = 1e-06


def side_by_side(arrays, axis, dim, along):
    widths = [a.shape[along] for a in arrays]
    both = jnp.concatenate(arrays, axis=along)
    whole = lax.all_gather(both, axis, axis=dim, tiled=True)
    return tuple(jnp.split(whole, [sum(widths[:k]) for k in range(1, len(widths))], axis=along))


def laid_out(parts, dim):
    dims = list(parts.shape[1:])
    dims[dim] *= parts.shape[0]
    return jnp.moveaxis(parts, 0, dim).reshape(dims)


def sent_to_all(shard, axis):
    copies = jnp.broadcast_to(shard, (lax.axis_size(axis), *shard.shape))
    return lax.all_to_all(copies, axis, split_axis=0, concat_axis=0, tiled=True)


def collect(shard, axis, dim):
    return laid_out(sent_to_all(shard, axis), dim)


def over_copies(shard, axis):
    everything = sent_to_all(shard, axis)
    return jnp.sum(everything, axis=0)


def of_everyone(shard, axis):
    everything = sent_to_all(shard, axis)
    return jnp.sum(everything.astype(jnp.float32), axis=0)


def in_blocks(shard, dim, count):
    dims = shard.shape
    parts = shard.reshape(*dims[:dim], count, dims[dim] // count, *dims[dim + 1 :])
    return jnp.moveaxis(parts, dim, 0)


def sent_and_summed(shard, axis, dim):
    count = lax.axis_size(axis)
    parts = lax.all_to_all(in_blocks(shard, dim, count), axis, 0, 0, tiled=True)
    return jnp.sum(parts.astype(jnp.float32), axis=0)


def encode_user(tokens, valid_len, w_uvqk, w_out, norm_gain):
    length, model_width = tokens.shape
    head_dim = model_width // HEADS
    projected = jnp.dot(tokens, w_uvqk, preferred_element_type=jnp.float32)
    activated = jax.nn.silu(projected)
    gate_part = activated[:, :model_width]
    values = activated[:, model_width : 2 * model_width].astype(jnp.bfloat16)
    queries = activated[:, 2 * model_width : 3 * model_width].astype(jnp.bfloat16)
    key_vecs = activated[:, 3 * model_width :].astype(jnp.bfloat16)
    key_heads = key_vecs.reshape(length, HEADS, head_dim)
    value_heads = values.reshape(length, HEADS, head_dim)
    block_rows = min(length, 512)
    columns = jnp.arange(length, dtype=jnp.int32)
    outputs = []
    for block_index in range(length // block_rows):
        query_heads = queries[block_index * block_rows : (block_index + 1) * block_rows]
        query_heads = query_heads.reshape(block_rows, HEADS, head_dim)
        scores = jnp.einsum(
            "ihd,jhd->hij", query_heads, key_heads, preferred_element_type=jnp.float32
        ) * head_dim ** (-0.5)
        rows_at = block_index * block_rows + jnp.arange(block_rows, dtype=jnp.int32)
        visible = (columns[None, :] <= rows_at[:, None]) & (columns[None, :] < valid_len)
        weights = jnp.where(visible[None], jax.nn.silu(scores), 0.0).astype(jnp.bfloat16)
        mixed_heads = jnp.einsum(
            "hij,jhd->ihd", weights, value_heads, preferred_element_type=jnp.float32
        )
        outputs.append(mixed_heads.reshape(block_rows, model_width))
    attended = jnp.concatenate(outputs, axis=0)
    inv_rms = lax.rsqrt(jnp.mean(attended * attended, axis=1, keepdims=True) + EPSILON)
    gated_out = (attended * inv_rms * norm_gain * gate_part).astype(jnp.bfloat16)
    return tokens.astype(jnp.float32) + jnp.dot(
        gated_out, w_out, preferred_element_type=jnp.float32
    )


def pool_sessions(enc_state, valid_len, sess_lens):
    length = enc_state.shape[0]
    sess_ends = jnp.cumsum(sess_lens)
    sess_starts = sess_ends - sess_lens
    positions = jnp.arange(length, dtype=jnp.int32)
    membership = (
        (positions[None, :] >= sess_starts[:, None])
        & (positions[None, :] < sess_ends[:, None])
        & (positions[None, :] < valid_len)
    ).astype(jnp.float32)
    sess_sums = jnp.dot(membership, enc_state)
    sess_counts = jnp.sum(membership, axis=1, keepdims=True)
    return (sess_sums / jnp.maximum(sess_counts, 1.0)).astype(jnp.bfloat16)


def per_device(events, hist_len, sess_len, w_uvqk, w_out, attn_gain, w_in, ffn_gain, w_up, w_down):
    full_uvqk, full_out = side_by_side((w_uvqk, w_out), "dp", 0, 1)
    enc_state = encode_user(events[0], hist_len[0], full_uvqk, full_out, attn_gain)
    pooled = pool_sessions(enc_state, hist_len[0], sess_len[0])
    micro_count = pooled.shape[0] // MICRO
    group_rows = collect(pooled[:micro_count], ("section", "mp"), 0)
    section_count = lax.axis_size("section")
    model_count = lax.axis_size("mp")
    total_rows = group_rows.shape[0]
    model_index = lax.axis_index("mp")
    local_in = jnp.dot(group_rows, w_in, preferred_element_type=jnp.float32)
    col_width = local_in.shape[1]
    square_sum = over_copies(jnp.sum(local_in * local_in, axis=1), ("section", "mp"))
    inv_rms = lax.rsqrt(square_sum / DM + EPSILON)
    normed_part = (local_in * inv_rms[:, None] * ffn_gain.astype(jnp.float32)).astype(jnp.bfloat16)
    half_up = jnp.dot(collect(normed_part, "mp", 1), w_up, preferred_element_type=jnp.float32)
    up_proj = of_everyone(half_up.astype(jnp.bfloat16), "section").astype(jnp.float32)
    hidden = jax.nn.gelu(up_proj, approximate=True).astype(jnp.bfloat16)
    unit_count = hidden.shape[1]
    hidden_order = hidden.reshape(section_count, model_count, micro_count, unit_count)
    hidden_order = hidden_order.transpose(1, 0, 2, 3).reshape(total_rows, unit_count)
    carry_order = local_in.reshape(section_count, model_count, micro_count, col_width)
    carry_order = carry_order.transpose(1, 0, 2, 3).reshape(total_rows, col_width)
    part_sum = jnp.dot(hidden_order, w_down, preferred_element_type=jnp.float32)
    target = lax.dynamic_slice_in_dim(part_sum, model_index * col_width, col_width, 1) + carry_order
    summed = sent_and_summed(
        lax.dynamic_update_slice_in_dim(part_sum, target, model_index * col_width, 1).astype(
            jnp.bfloat16
        ),
        "mp",
        0,
    )
    full_rows = lax.all_to_all(
        summed.astype(jnp.bfloat16), "section", split_axis=0, concat_axis=1, tiled=True
    ).astype(summed.dtype)
    cross_out = full_rows.astype(jnp.bfloat16)
    return (pooled, cross_out)


def solution(mesh):
    return jax.shard_map(
        per_device,
        mesh=mesh,
        in_specs=(
            P(("section", "dp", "mp"), None, None),
            P(("section", "dp", "mp")),
            P(("section", "dp", "mp"), None),
            P("dp", None),
            P("dp", None),
            P(),
            P(None, ("section", "mp")),
            P(None, ("section", "mp")),
            P("section", "mp"),
            P("mp", "section"),
        ),
        out_specs=(P(("section", "dp", "mp"), None), P(("section", "dp", "mp"), None)),
        check_vma=False,
    )
```

profile of v0, /device:TPU:1, one launch (start us, length us, event | category | flops | bytes accessed | tf_op | source)
XLA Modules:
  0.0 210.0 jit_solution(9146511009298793382)
XLA Ops:
  7.2 1.7 pad_maximum_fusion.1
  9.6 0.7 copy.41
  10.6 0.7 bitcast_subtract_fusion
  11.4 1.5 fusion.15
  13.0 67.1 %all-gather.2.cloned.1.call-done = bf16[512,2560]{1,0:T(8,128)(2,1)} async-done(((bf16[32,2560]{1,0:T(8,128)(2,1)}), bf16[512,2560]{1,0:T(8,128)(2,1)}) %all-gather.2.cloned.1.call-update) | async-done | bytes 2621456 | tf_op jit(solution)/shard_map/all_gather | solution.py:17
  80.0 9.1 %fusion.64 = (bf16[1024,2048]{0,1:T(8,128)(2,1)S(1)}, f32[1024,2048]{0,1:T(8,128)}) fusion(bf16[1,1024,512]{2,1,0:T(8,128)(2,1)} %param.10, bf16[512,2560]{1,0:T(8,128)(2,1)} %all-gather.2.cloned.1.call-done), kind=kOutput, calls=%fused_computation.75 | convolution fusion | flops 2157969408 | bytes 15728640 | tf_op jit(solution)/shard_map/dot_general | solution.py:61
  89.1 1.5 fusion.63
  90.6 1.0 fusion.62
  91.7 5.9 %fusion.3 = f32[4,128,512]{2,1,0:T(8,128)S(1)} fusion(bf16[1024,4,128]{0,2,1:T(8,128)(2,1)} %bitcast.82, pred[512,1024]{1,0:T(8,128)(4,1)} %get-tuple-element.6, bf16[512,4,128]{0,2,1:T(8,128)(2,1)} %bitcast.85, bf16[1024,4,128]{0,2,1:T(8,128)(2,1)} %bitcast.80), kind=kOutput, calls=%fused_computation.7 | convolution fusion | flops 1088421888 | bytes 4194304 | tf_op jit(solution)/shard_map/hij,jhd->ihd/dot_general | solution.py:81
  97.6 7.0 %fusion.4 = f32[4,128,512]{2,1,0:T(8,128)} fusion(bf16[1024,4,128]{0,2,1:T(8,128)(2,1)} %bitcast.83, pred[512,1024]{1,0:T(8,128)(4,1)} %get-tuple-element.7, bf16[512,4,128]{0,2,1:T(8,128)(2,1)} %bitcast.84, bf16[1024,4,128]{0,2,1:T(8,128)(2,1)} %bitcast.81), kind=kOutput, calls=%fused_computation.8 | convolution fusion | flops 1088421888 | bytes 4194304 | tf_op jit(solution)/shard_map/hij,jhd->ihd/dot_general | solution.py:81
  104.6 1.4 multiply_reduce_fusion
  106.1 3.5 %fusion.24 = bf16[32,512]{1,0:T(8,128)(2,1)S(1)} fusion(f32[1024,2048]{0,1:T(8,128)} %get-tuple-element.9, f32[512,512]{0,1:T(8,128)} %bitcast.79, f32[512,512]{0,1:T(8,128)S(1)} %bitcast.77, bf16[1,1024,512]{2,1,0:T(8,128)(2,1)} %param.10, f32[512]{0:T(512)S(1)} %copy-done.3, f32[1024]{0:T(1024)S(1)} %add_rsqrt_fusion, ...), kind=kOutput, calls=%fused_computation.27 | convolution fusion | flops 574259200 | bytes 5807488 | tf_op jit(solution)/shard_map/dot_general | solution.py:103
  109.7 25.2 %all_to_all.45 = bf16[32,8,512]{2,1,0:T(8,128)(2,1)S(1)} all-to-all(bf16[32,8,512]{2,1,0:T(8,128)(2,1)S(1)} %broadcast_in_dim.50), channel_id=1, replica_groups=mesh['section'=2,'dp'=16,'mp'=16] {'section','mp'}, dimensions={0} | all-to-all | bytes 524288 | tf_op jit(solution)/shard_map/all_to_all | solution.py:29
  135.1 0.6 broadcast_in_dim.51
  135.8 4.6 %all-to-all-start.1 = ((f32[32,1,256]{2,1,0:T(1,128)}), f32[32,1,256]{2,1,0:T(1,128)S(1)}, u32[]{:S(2)}, u32[]{:S(2)}) async-start(f32[32,1,256]{2,1,0:T(1,128)} %broadcast_in_dim.51), calls=%async_computation.1 | async-start | bytes 65536 | tf_op jit(solution)/shard_map/all_to_all | solution.py:29
  140.4 7.0 %all-to-all-done.1 = f32[32,1,256]{2,1,0:T(1,128)S(1)} async-done(((f32[32,1,256]{2,1,0:T(1,128)}), f32[32,1,256]{2,1,0:T(1,128)S(1)}, u32[]{:S(2)}, u32[]{:S(2)}) %all-to-all-start.1) | async-done | bytes 32800 | tf_op jit(solution)/shard_map/all_to_all | solution.py:29
  147.7 1.1 broadcast_in_dim.52
  148.7 3.7 %all-to-all-start.2 = ((bf16[16,256,128]{1,2,0:T(8,128)(2,1)}), bf16[16,256,128]{1,2,0:T(8,128)(2,1)S(1)}, u32[]{:S(2)}, u32[]{:S(2)}) async-start(bf16[16,256,128]{1,2,0:T(8,128)(2,1)} %broadcast_in_dim.52), calls=%async_computation.2 | async-start | bytes 2097152 | tf_op jit(solution)/shard_map/all_to_all | solution.py:29
  152.4 16.3 %all-to-all-done.2 = bf16[16,256,128]{1,2,0:T(8,128)(2,1)S(1)} async-done(((bf16[16,256,128]{1,2,0:T(8,128)(2,1)}), bf16[16,256,128]{1,2,0:T(8,128)(2,1)S(1)}, u32[]{:S(2)}, u32[]{:S(2)}) %all-to-all-start.2) | async-done | bytes 1048608 | tf_op jit(solution)/shard_map/all_to_all | solution.py:29
  168.8 2.3 %convolution_convert_fusion = bf16[256,512]{1,0:T(8,128)(2,1)S(1)} fusion(bf16[256,2048]{0,1:T(8,128)(2,1)S(1)} %bitcast.75, bf16[2048,512]{1,0:T(8,128)(2,1)} %param.18), kind=kOutput, calls=%fused_computation.25 | convolution fusion | flops 537001984 | bytes 3407872 | tf_op jit(solution)/shard_map/dot_general | solution.py:123
  171.1 5.8 %all_to_all.46 = bf16[2,256,512]{2,1,0:T(8,128)(2,1)S(1)} all-to-all(bf16[2,256,512]{2,1,0:T(8,128)(2,1)S(1)} %broadcast_in_dim.53), channel_id=1, replica_groups=mesh['section'=2,'dp'=16,'mp'=16] {'section'}, dimensions={0} | all-to-all | bytes 1048576 | tf_op jit(solution)/shard_map/all_to_all | solution.py:29
  177.2 0.7 fusion.65
  178.2 19.1 %all_to_all.47 = bf16[16,16,2048]{2,1,0:T(8,128)(2,1)S(1)} all-to-all(bf16[16,16,2048]{2,1,0:T(8,128)(2,1)S(1)} %bitcast.71), channel_id=1, replica_groups=mesh['section'=2,'dp'=16,'mp'=16] {'mp'}, dimensions={0} | all-to-all | bytes 2097152 | tf_op jit(solution)/shard_map/all_to_all | solution.py:54
  197.4 5.2 %all_to_all.48 = bf16[2,8,2048]{2,1,0:T(8,128)(2,1)S(1)} all-to-all(bf16[2,8,2048]{2,1,0:T(8,128)(2,1)S(1)} %bitcast.86), channel_id=1, replica_groups=mesh['section'=2,'dp'=16,'mp'=16] {'section'}, dimensions={0} | all-to-all | bytes 131072 | tf_op jit(solution)/shard_map/all_to_all | solution.py:140
  (36 shorter events, 2.4 us)
Async XLA Ops:
  7.2 170.1 %copy-start = (bf16[512,2048]{1,0:T(8,128)(2,1)S(1)}, bf16[512,2048]{1,0:T(8,128)(2,1)}, u32[]{:S(2)}) copy-start(bf16[512,2048]{1,0:T(8,128)(2,1)} %param.19) | copy-start | bytes 6291460
  7.2 72.9 %all-gather.2.cloned.1.call-start = ((), (), s32[]{:S(2)}) async-start(), calls=%async_computation.6 | async-start | bytes 2785280 | tf_op jit(solution)/shard_map/all_gather | solution.py:17
  97.6 8.5 %copy-start.3 = (f32[512]{0:T(512)S(1)}, f32[512]{0:T(512)}, u32[]{:S(2)}) copy-start(f32[512]{0:T(512)} %param.15) | copy-start | bytes 6148
  106.0 28.8 %copy-start.1 = (bf16[512,128]{1,0:T(8,128)(2,1)S(1)}, bf16[512,128]{1,0:T(8,128)(2,1)}, u32[]{:S(2)}) copy-start(bf16[512,128]{1,0:T(8,128)(2,1)} %param.16) | copy-start | bytes 393220
  106.1 34.3 %copy-start.4 = (bf16[1,128]{1,0:T(2,128)(2,1)S(1)}, bf16[1,128]{1,0:T(2,128)(2,1)}, u32[]{:S(2)}) copy-start(bf16[1,128]{1,0:T(2,128)(2,1)} %param.17) | copy-start | bytes 772
  109.6 42.8 %copy-start.2 = (bf16[32,512]{1,0:T(8,128)(2,1)}, bf16[32,512]{1,0:T(8,128)(2,1)S(1)}, u32[]{:S(2)}) copy-start(bf16[32,512]{1,0:T(8,128)(2,1)S(1)} %fusion.24) | copy-start | bytes 98308
  135.8 11.6 %all-to-all-start.1 = ((f32[32,1,256]{2,1,0:T(1,128)}), f32[32,1,256]{2,1,0:T(1,128)S(1)}, u32[]{:S(2)}, u32[]{:S(2)}) async-start(f32[32,1,256]{2,1,0:T(1,128)} %broadcast_in_dim.51), calls=%async_computation.1 | async-start | bytes 65536 | tf_op jit(solution)/shard_map/all_to_all | solution.py:29
  148.7 20.0 %all-to-all-start.2 = ((bf16[16,256,128]{1,2,0:T(8,128)(2,1)}), bf16[16,256,128]{1,2,0:T(8,128)(2,1)S(1)}, u32[]{:S(2)}, u32[]{:S(2)}) async-start(bf16[16,256,128]{1,2,0:T(8,128)(2,1)} %broadcast_in_dim.52), calls=%async_computation.2 | async-start | bytes 2097152 | tf_op jit(solution)/shard_map/all_to_all | solution.py:29
Sparse Core Ops, SparseCore 0:
  10.1 69.9 all-gather.1
where the time goes:
time: 211 us; the launch traced here: 210 us
  waiting for transfers between devices  90.4 us (43%)
  blocking collectives  55.3 us (26%)
  matrix products  28.8 us (14%)
  between operations  14.9 us (7%)
  starting transfers between devices  8.3 us (4%)
  other arithmetic  6.5 us (3%)
  local copies, waits for them, and re-layouts  5.9 us (3%)
    all_gather x1, waiting for transfers between devices, side_by_side(): whole = lax.all_gather(both, axis, axis=dim, tiled=True)  67.1 us
    all_to_all x2, blocking collectives, sent_to_all(): return lax.all_to_all(copies, axis, split_axis=0, concat_axis=0, tiled=True)  31 us
    all_to_all x2, waiting for transfers between devices, sent_to_all(): return lax.all_to_all(copies, axis, split_axis=0, concat_axis=0, tiled=True)  23.3 us
    all_to_all x1, blocking collectives, sent_and_summed(): parts = lax.all_to_all(in_blocks(shard, dim, count), axis, 0, 0, tiled=True)  19.1 us
    dot_general x2, matrix products, encode_user(): jnp.einsum('hij,jhd->ihd', weights, value_heads, preferred_element_type=j...  12.9 us
    dot_general x1, matrix products, encode_user(): projected = jnp.dot(tokens, w_uvqk, preferred_element_type=jnp.float32)  9.08 us
    all_to_all x2, starting transfers between devices, sent_to_all(): return lax.all_to_all(copies, axis, split_axis=0, concat_axis=0, tiled=True)  8.27 us
    all_to_all x1, blocking collectives, per_device(): lax.all_to_all(summed.astype(jnp.bfloat16), 'section', split_axis=0, conc...  5.21 us
  transfers between devices with their start and end apart: 3, of which 3 were waited for; matrix products, arithmetic and copies ran while one was open for 2% of the time, Pallas kernels for 0%

commit v1 on v0

v1 whole, which is shorter than its diff:
```python
import jax
import jax.numpy as jnp
from jax import lax
from jax.experimental import pallas as pl
from jax.experimental.pallas import tpu as pltpu
from jax.sharding import PartitionSpec as P

MESH = pl.DeviceIdType.MESH
BF = jnp.bfloat16
F32 = jnp.float32
EPSILON = 1e-06
DMA = pltpu.SemaphoreType.DMA


def dot(a, b):
    return jnp.dot(a, b, preferred_element_type=F32)


def dot_nt(a, b):
    return lax.dot_general(a, b, (((1,), (1,)), ((), ())), preferred_element_type=F32)


def silu(v):
    half = 0.5 * v
    return half + half * jnp.tanh(half)


def kernel(
    events, hist, sess, w_uvqk, w_out, gain, w_in, ffn_gain, w_up, w_down,
    pooled_out, cross_out,
    ev, wa, wo, wi, wu, wd, qs, ks, vs, gs, att, gated, member, rows, hin, part, recv, parts,
    loc, z_s, z_r, zo_s, zo_r, a1_s, a1_r, ao_s, ao_r, a2_s, a2_r, pa_s, pa_r, po_s, po_r,
    b1_s, b1_r, b2_s, b2_r, pb_s, pb_r, pw_s, pw_r, r_s, r_r, c_s, c_r,
):
    s = lax.axis_index("section")
    z = lax.axis_index("dp")
    m = lax.axis_index("mp")
    x = lax.rem(m, 4)
    y = m // 4
    first = (1 - s) * x + s * y
    partner = (1 - s, z, m)

    def spot(d, e):
        xx = lax.rem(x + (1 - s) * d + s * e, 4)
        yy = lax.rem(y + s * d + (1 - s) * e, 4)
        return yy * 4 + xx

    def remote(src, dst, ss, rs, to):
        return pltpu.make_async_remote_copy(
            src_ref=src, dst_ref=dst, send_sem=ss, recv_sem=rs, device_id=to, device_id_type=MESH
        )

    col_a = pl.ds(pl.multiple_of(m * 128, 128), 128)
    col_o = pl.ds(pl.multiple_of(first * 128, 128), 128)
    locals_ = [
        pltpu.make_async_copy(w_uvqk.at[s, :, col_a], wa.at[z, s, :, col_a], loc.at[0]),
        pltpu.make_async_copy(w_out.at[s, :, col_o], wo.at[z, s, :, col_o], loc.at[1]),
        pltpu.make_async_copy(events.at[0], ev, loc.at[2]),
        pltpu.make_async_copy(w_in, wi.at[pl.ds(0, 512), pl.ds((16 * s + m) * 128, 128)], loc.at[3]),
        pltpu.make_async_copy(w_up, wu.at[s], loc.at[4]),
        pltpu.make_async_copy(w_down, wd.at[s], loc.at[5]),
    ]
    for c in locals_:
        c.start()

    barrier = pltpu.get_barrier_semaphore()

    @pl.loop(1, 16)
    def _(d):
        pl.semaphore_signal(barrier, inc=1, device_id=(s, lax.rem(z + d, 16), m), device_id_type=MESH)
        pl.semaphore_signal(barrier, inc=1, device_id=(s, z, lax.rem(m + d, 16)), device_id_type=MESH)

    pl.semaphore_signal(barrier, inc=1, device_id=partner, device_id_type=MESH)

    mine = pl.ds(pl.multiple_of((16 * s + m) * 128, 128), 128)
    wi[pl.ds(512, 16), mine] = jnp.broadcast_to(ffn_gain[...], (16, 128))

    lens = jnp.broadcast_to(sess[...], (32, 32))
    at = lax.broadcasted_iota(jnp.int32, (32, 32), 0)
    of = lax.broadcasted_iota(jnp.int32, (32, 32), 1)
    ends = jnp.sum(jnp.where(of <= at, lens, 0).astype(F32), axis=1, keepdims=True)
    starts = jnp.sum(jnp.where(of < at, lens, 0).astype(F32), axis=1, keepdims=True)
    pos = lax.broadcasted_iota(jnp.int32, (32, 1024), 1).astype(F32)
    limit = jnp.minimum(ends, jnp.broadcast_to(hist[...], (32, 1)).astype(F32))
    inside = (pos >= starts) & (pos < limit)
    member[...] = jnp.where(inside, 1.0, 0.0).astype(BF)
    counts = jnp.maximum(limit - starts, 1.0)

    locals_[0].wait()
    locals_[1].wait()
    pl.semaphore_wait(barrier, 31)


    def z_copy(src_z, d, to_z):
        return remote(
            wa.at[src_z, s, :, col_a], wa.at[src_z, s, :, col_a], z_s.at[d], z_r.at[src_z], (s, to_z, m)
        )

    def zo_copy(src_z, d, to_z):
        return remote(
            wo.at[src_z, s, :, col_o], wo.at[src_z, s, :, col_o], zo_s.at[d], zo_r.at[src_z], (s, to_z, m)
        )

    @pl.loop(1, 16)
    def _(d):
        to = lax.rem(z + d, 16)
        z_copy(z, d, to).start()
        zo_copy(z, d, to).start()

    pw = [
        remote(w_up, wu.at[s], pw_s.at[0], pw_r.at[0], partner),
        remote(w_down, wd.at[s], pw_s.at[1], pw_r.at[1], partner),
    ]
    for c in pw:
        c.start()

    home, inner = z // 4, lax.rem(z, 4)
    step = 1 - 2 * ((5 - inner) // 4)
    groups = [home, lax.rem(home + step + 4, 4), lax.rem(home - step + 4, 4), lax.rem(home + 2, 4)]

    def block(g, mm):
        return wa.at[pl.ds(4 * g, 4), s, :, pl.ds(pl.multiple_of(mm * 128, 128), 128)]

    def oblock(g, ff):
        return wo.at[pl.ds(4 * g, 4), s, :, pl.ds(pl.multiple_of(ff * 128, 128), 128)]

    def a1(i, d):
        b = block(groups[i], m)
        return remote(b, b, a1_s.at[i, d - 1], a1_r.at[i, d - 1], (s, z, spot(d, 0)))

    def ao(i, d):
        b = oblock(groups[i], first)
        return remote(b, b, ao_s.at[i, d - 1], ao_r.at[i, d - 1], (s, z, spot(d, 0)))

    def a1_got(i, d):
        b = block(groups[i], spot(4 - d, 0))
        return remote(b, b, a1_s.at[i, d - 1], a1_r.at[i, d - 1], partner)

    def ao_got(i, d):
        b = oblock(groups[i], lax.rem(first + 4 - d, 4))
        return remote(b, b, ao_s.at[i, d - 1], ao_r.at[i, d - 1], partner)

    def a2(i, d, e):
        b = block(groups[i], spot(4 - d, 0))
        return remote(b, b, a2_s.at[i, d, e - 1], a2_r.at[i, d, e - 1], (s, z, spot(0, e)))

    def a2_got(i, d, e):
        b = block(groups[i], spot(4 - d, 4 - e))
        return remote(b, b, a2_s.at[i, d, e - 1], a2_r.at[i, d, e - 1], partner)

    for i in range(4):
        g = groups[i]
        for k in range(1 if i == 0 else 0, 4):
            src = 4 * g + (lax.rem(inner + k, 4) if i == 0 else k)
            z_copy(src, 0, z).wait_recv()
            zo_copy(src, 0, z).wait_recv()
        for d in range(1, 4):
            a1(i, d).start()
            ao(i, d).start()
        for e in range(1, 4):
            a2(i, 0, e).start()

    def pa(i, side):
        b = wa.at[pl.ds(4 * groups[i], 4), side]
        return remote(b, b, pa_s.at[i], pa_r.at[i], partner)

    def po(i, side):
        b = wo.at[pl.ds(4 * groups[i], 4), side]
        return remote(b, b, po_s.at[i], po_r.at[i], partner)

    for i in range(4):
        for d in range(1, 4):
            a1_got(i, d).wait_recv()
            for e in range(1, 4):
                a2(i, d, e).start()
        for d in range(1, 4):
            ao_got(i, d).wait_recv()
        po(i, s).start()

    locals_[3].wait()

    def win(mm, side):
        return wi.at[:, pl.ds(pl.multiple_of((16 * side + mm) * 128, 128), 128)]

    def b1(d):
        b = win(m, s)
        return remote(b, b, b1_s.at[d - 1], b1_r.at[d - 1], (s, z, spot(d, 0)))

    def b1_got(d):
        b = win(spot(4 - d, 0), s)
        return remote(b, b, b1_s.at[d - 1], b1_r.at[d - 1], partner)

    def b2(d, e):
        b = win(spot(4 - d, 0), s)
        return remote(b, b, b2_s.at[d, e - 1], b2_r.at[d, e - 1], (s, z, spot(0, e)))

    def b2_got(d, e):
        b = win(spot(4 - d, 4 - e), s)
        return remote(b, b, b2_s.at[d, e - 1], b2_r.at[d, e - 1], partner)

    def pb(side):
        b = wi.at[:, pl.ds(pl.multiple_of(side * 2048, 128), 2048)]
        return remote(b, b, pb_s, pb_r, partner)

    for d in range(1, 4):
        b1(d).start()
    for e in range(1, 4):
        b2(0, e).start()

    for i in range(4):
        for d in range(4):
            for e in range(1, 4):
                a2_got(i, d, e).wait_recv()
        pa(i, s).start()

    for d in range(1, 4):
        b1_got(d).wait_recv()
        for e in range(1, 4):
            b2(d, e).start()

    locals_[2].wait()
    for i in range(4):
        pa(i, 1 - s).wait_recv()
        po(i, 1 - s).wait_recv()

    valid = jnp.broadcast_to(hist[...], (256, 1))

    def project(r):
        at_rows = pl.ds(pl.multiple_of(r * 256, 256), 256)
        tokens = ev[at_rows, :]
        row = r * 256 + lax.broadcasted_iota(jnp.int32, (256, 1), 0)

        def part_of(c):
            w = wa[:, :, :, pl.ds(512 * c, 512)].reshape(512, 512)
            return silu(dot(tokens, w))

        gs[at_rows, :] = part_of(0)
        vs[at_rows, :] = jnp.where(row < valid, part_of(1), 0.0).astype(BF)
        qs[at_rows, :] = (part_of(2) * (0.5 * 128 ** (-0.5))).astype(BF)
        ks[at_rows, :] = part_of(3).astype(BF)

    def attend(i):
        lo = i * 256
        diagonal = lax.broadcasted_iota(jnp.int32, (256, 256), 1) <= lax.broadcasted_iota(
            jnp.int32, (256, 256), 0
        )

        @pl.loop(0, 4)
        def _(h):
            cols = pl.ds(pl.multiple_of(h * 128, 128), 128)
            q = qs[pl.ds(lo, 256), cols]

            def weigh(j):
                u = dot_nt(q, ks[pl.ds(256 * j, 256), cols])
                return u + u * jnp.tanh(u)

            acc = dot(
                jnp.where(diagonal, weigh(i), 0.0).astype(BF), vs[pl.ds(lo, 256), cols]
            )
            for j in range(i):
                acc += dot(weigh(j).astype(BF), vs[pl.ds(256 * j, 256), cols])
            att[pl.ds(lo, 256), cols] = acc

    def gate(i):
        at_rows = pl.ds(i * 256, 256)
        a = att[at_rows, :]
        inv = lax.rsqrt(jnp.mean(a * a, axis=1, keepdims=True) + EPSILON)
        gated[at_rows, :] = (a * inv * gain[...] * gs[at_rows, :]).astype(BF)

    def pool(r0, nr, upto):
        mm = member[pl.ds(r0, nr), pl.ds(0, upto)]
        pe = dot(mm, ev[pl.ds(0, upto), :])
        pg = dot(mm, gated[pl.ds(0, upto), :])
        hi = pg.astype(BF)
        lo = (pg - hi.astype(F32)).astype(BF)
        w = wo[...].reshape(512, 512)
        return pe + dot(hi, w) + dot(lo, w)

    for r in range(2):
        project(r)
    for i in range(2):
        attend(i)
        gate(i)
    early = (pool(0, 16, 512) / counts[0:16])[0:8].astype(BF)
    rows[m] = early

    def r_copy(d, slot, to):
        return remote(rows.at[slot], rows.at[slot], r_s.at[d], r_r.at[d], (s, z, to))

    @pl.loop(1, 16)
    def _(d):
        r_copy(d, m, lax.rem(m + d, 16)).start()

    for r in range(2, 4):
        project(r)
    for i in range(2, 4):
        attend(i)
        gate(i)
    parts[...] = pool(0, 32, 1024) / counts
    pooled_out[...] = parts[...].astype(BF)

    for d in range(4):
        for e in range(1, 4):
            b2_got(d, e).wait_recv()
    pb(s).start()

    @pl.loop(1, 16)
    def _(d):
        r_copy(d, lax.rem(m + 16 - d, 16), m).wait_recv()

    locals_[4].wait()
    locals_[5].wait()
    for k, c in enumerate(pw):
        c.wait_recv()
    pb(1 - s).wait_recv()

    xs = rows[...].astype(F32).reshape(128, 512).astype(BF)

    def widen(c, carry):
        acc, sq = carry
        cols = pl.ds(pl.multiple_of(c * 512, 512), 512)
        h = dot(xs, wi[pl.ds(0, 512), cols])
        hin[:, cols] = h
        g = wi[pl.ds(512, 16), cols].astype(F32)[0:1]
        at_k = pl.ds(pl.multiple_of(lax.rem(c, 4) * 512, 512), 512)
        acc += dot((h * g).astype(BF), wu[c // 4, at_k, :])
        return acc, sq + jnp.sum(h * h, axis=1, keepdims=True)

    acc, sq = lax.fori_loop(
        0, 8, widen, (jnp.zeros((128, 512), F32), jnp.zeros((128, 1), F32))
    )
    up = acc * lax.rsqrt(sq * (1.0 / 4096) + EPSILON)
    hidden = jax.nn.gelu(up, approximate=True).astype(BF)

    def c_copy(half, d, src, dst, to):
        cols = pl.ds(half * 2048, 2048)
        return remote(
            part.at[src, :, cols], recv.at[dst, :, cols], c_s.at[half, d], c_r.at[half, d], (s, z, to)
        )

    for half in range(2):

        @pl.loop(0, 4)
        def _(c):
            cols = pl.ds(pl.multiple_of(half * 2048 + c * 512, 512), 512)
            p = dot(hidden, wd[half, :, pl.ds(pl.multiple_of(c * 512, 512), 512)])
            part[:, :, cols] = p.reshape(16, 8, 512).astype(BF)

        @pl.loop(1, 16)
        def _(d):
            to = lax.rem(m + d, 16)
            c_copy(half, d, to, m, to).start()

    for half in range(2):
        cols = pl.ds(half * 2048, 2048)
        total = hin[pl.ds(pl.multiple_of(m * 8, 8), 8), cols] + part[m, :, cols].astype(F32)

        def gather(d, total):
            src = lax.rem(m + 16 - d, 16)
            c_copy(half, d, 0, src, m).wait_recv()
            return total + recv[src, :, cols].astype(F32)

        total = lax.fori_loop(1, 16, gather, total)
        cross_out[:, cols] = total.astype(BF)

    @pl.loop(1, 16)
    def _(d):
        z_copy(z, d, z).wait_send()
        zo_copy(z, d, z).wait_send()
        r_copy(d, m, m).wait_send()
        c_copy(0, d, 0, m, m).wait_send()
        c_copy(1, d, 0, m, m).wait_send()

    for c in pw:
        c.wait_send()
    for i in range(4):
        for d in range(1, 4):
            a1(i, d).wait_send()
            ao(i, d).wait_send()
        for d in range(4):
            for e in range(1, 4):
                a2(i, d, e).wait_send()
        pa(i, s).wait_send()
        po(i, s).wait_send()
    for d in range(1, 4):
        b1(d).wait_send()
    for d in range(4):
        for e in range(1, 4):
            b2(d, e).wait_send()
    pb(s).wait_send()


def per_device(events, hist_len, sess_len, w_uvqk, w_out, attn_gain, w_in, ffn_gain, w_up, w_down):
    anywhere = pl.BlockSpec(memory_space=pl.ANY)
    inside = pl.BlockSpec(memory_space=pltpu.VMEM)
    vm = pltpu.VMEM
    return pl.pallas_call(
        kernel,
        out_shape=(jax.ShapeDtypeStruct((32, 512), BF), jax.ShapeDtypeStruct((8, 4096), BF)),
        in_specs=[
            anywhere, inside, inside, anywhere, anywhere, inside, anywhere, inside, anywhere, anywhere,
        ],
        out_specs=(inside, inside),
        scratch_shapes=[
            vm((1024, 512), BF),
            vm((16, 2, 16, 2048), BF),
            vm((16, 2, 16, 512), BF),
            vm((528, 4096), BF),
            vm((2, 2048, 512), BF),
            vm((2, 512, 2048), BF),
            vm((1024, 512), BF),
            vm((1024, 512), BF),
            vm((1024, 512), BF),
            vm((1024, 512), F32),
            vm((1024, 512), F32),
            vm((1024, 512), BF),
            vm((32, 1024), BF),
            vm((16, 8, 512), BF),
            vm((128, 4096), F32),
            vm((16, 8, 4096), BF),
            vm((16, 8, 4096), BF),
            vm((32, 512), F32),
            DMA((6,)),
            DMA((16,)), DMA((16,)), DMA((16,)), DMA((16,)),
            DMA((4, 3)), DMA((4, 3)), DMA((4, 3)), DMA((4, 3)),
            DMA((4, 4, 3)), DMA((4, 4, 3)),
            DMA((4,)), DMA((4,)), DMA((4,)), DMA((4,)),
            DMA((3,)), DMA((3,)), DMA((4, 3)), DMA((4, 3)),
            DMA, DMA,
            DMA((2,)), DMA((2,)),
            DMA((16,)), DMA((16,)),
            DMA((2, 16)), DMA((2, 16)),
        ],
        compiler_params=pltpu.CompilerParams(
            collective_id=0, has_side_effects=True, vmem_limit_bytes=60 << 20
        ),
        name="encode_and_mix",
    )(
        events, hist_len.reshape(1, 1), sess_len, w_uvqk.reshape(2, 16, 2048), w_out.reshape(2, 16, 512),
        attn_gain.reshape(1, 512), w_in, ffn_gain, w_up, w_down,
    )


def solution(mesh):
    return jax.shard_map(
        per_device,
        mesh=mesh,
        in_specs=(
            P(("section", "dp", "mp"), None, None),
            P(("section", "dp", "mp")),
            P(("section", "dp", "mp"), None),
            P("dp", None),
            P("dp", None),
            P(),
            P(None, ("section", "mp")),
            P(None, ("section", "mp")),
            P("section", "mp"),
            P("mp", "section"),
        ),
        out_specs=(P(("section", "dp", "mp"), None), P(("section", "dp", "mp"), None)),
        check_vma=False,
    )
```

time: 211 us -> 84.3 us (0.40)
  waiting for transfers between devices: 90.4 us -> 0 us
  Pallas kernels: 0 us -> 79.9 us
  blocking collectives: 55.3 us -> 0 us
  matrix products: 28.8 us -> 0 us
  between operations: 14.9 us -> 1.29 us
  starting transfers between devices: 8.3 us -> 0 us
  other arithmetic: 6.5 us -> 0 us
  local copies, waits for them, and re-layouts: 5.9 us -> 2.85 us
    pallas_call x0 -> x1, Pallas kernels: none -> 79.9 us  [per_device(): pl.pallas_call(kernel, out_shape=(jax.ShapeDtypeStruct((32, 512), BF), ja...]
    all_gather x1 -> x0, waiting for transfers between devices: 67.1 us -> none  [side_by_side(): whole = lax.all_gather(both, axis, axis=dim, tiled=True)]
    all_to_all x4 -> x0, blocking collectives: 55.3 us -> none  [the longest x2 31 us: sent_to_all(): return lax.all_to_all(copies, axis, split_axis=0, concat_axis=0, tiled=True)]
    dot_general x7 -> x0, matrix products: 28.8 us -> none  [the longest x2 12.9 us: encode_user(): jnp.einsum('hij,jhd->ihd', weights, value_heads, preferred_element_type=j...]
    all_to_all x2 -> x0, waiting for transfers between devices: 23.3 us -> none  [sent_to_all(): return lax.all_to_all(copies, axis, split_axis=0, concat_axis=0, tiled=True)]
    all_to_all x2 -> x0, starting transfers between devices: 8.27 us -> none  [sent_to_all(): return lax.all_to_all(copies, axis, split_axis=0, concat_axis=0, tiled=True)]
    slice x3 -> x0, local copies, waits for them, and re-layouts: 2.57 us -> none  [the longest x1 1.52 us: encode_user(): key_vecs = activated[:, 3 * model_width:].astype(jnp.bfloat16)]
    unnamed x11 -> x2, local copies, waits for them, and re-layouts: 0.66 us -> 2.85 us
  transfers between devices with their start and end apart: 3 -> 0, of which waited for: 3 -> 0; matrix products, arithmetic and copies ran while one was open for 2% -> 0% of each run, Pallas kernels for 0% -> 0%
where the time goes in v1:
time: 84.3 us; the launch traced here: 84 us
  Pallas kernels  79.9 us (95%)
  local copies, waits for them, and re-layouts  2.85 us (3%)
  between operations  1.29 us (2%)
    pallas_call x1, Pallas kernels, per_device(): pl.pallas_call(kernel, out_shape=(jax.ShapeDtypeStruct((32, 512), BF), ja...  79.9 us
    unnamed x2, local copies, waits for them, and re-layouts  2.85 us

profile of v1, /device:TPU:1, one launch (start us, length us, event | category | flops | bytes accessed | tf_op | source)
XLA Modules:
  0.0 84.0 jit_solution(1448265736284678111)
XLA Ops:
  1.3 79.9 %encode_and_mix.1 = (bf16[32,512]{1,0:T(8,128)(2,1)}, bf16[8,4096]{1,0:T(8,128)(2,1)}) custom-call(bf16[1,1024,512]{2,1,0:T(8,128)(2,1)} %events.1, s32[1,1]{1,0:T(1,128)} %bitcast.4.hist, s32[1,32]{1,0:T(1,128)} %sess.1, bf16[2,16,2048]{2,1,0:T(8,128)(2,1)} %bitcast.5, bf16[2,16,512]{2,1,0:T(8,128)(2,1)} %bitcast.6, f32[1,512]{1,0:T(1,128)} %bitcast.7, ...), custom_call_target="tpu_custom_call" | custom-call | tf_op jit(solution)/shard_map/encode_and_mix/pallas_call | solution.py:397
  81.2 1.4 %copy.15 = bf16[32,512]{1,0:T(8,128)(2,1)} copy(bf16[32,512]{1,0:T(8,128)(2,1)} %get-tuple-element.4) | data formatting | bytes 65536
  82.6 1.5 %copy.16 = bf16[8,4096]{1,0:T(8,128)(2,1)} copy(bf16[8,4096]{1,0:T(8,128)(2,1)} %get-tuple-element.5) | data formatting | bytes 131072

commit v2 on v1

v2 whole, which is shorter than its diff:
```python
import jax
import jax.numpy as jnp
from jax import lax
from jax.experimental import pallas as pl
from jax.experimental.pallas import tpu as pltpu
from jax.sharding import PartitionSpec as P

MESH = pl.DeviceIdType.MESH
BF = jnp.bfloat16
F32 = jnp.float32
EPSILON = 1e-06
DMA = pltpu.SemaphoreType.DMA


def dot(a, b):
    return jnp.dot(a, b, preferred_element_type=F32)


def dot_nt(a, b):
    return lax.dot_general(a, b, (((1,), (1,)), ((), ())), preferred_element_type=F32)


def silu(v):
    half = 0.5 * v
    return half + half * jnp.tanh(half)


def kernel(
    events, hist, sess, w_uvqk, w_out, gain, w_in, ffn_gain, w_up, w_down,
    pooled_out, cross_out,
    hist_v, sess_v, gain_v, fgain_v, pooled_v, cross_v,
    ev, wa, wo, wi, wu, wd, qs, ks, vs, gs, att, gated, member, rows, hin, part, recv, relay, last, own,
    pre, loc, z_s, z_r, zo_s, zo_r, a1_s, a1_r, ao_s, ao_r, a2_s, a2_r, pa_s, pa_r, po_s, po_r,
    b_s, f_s, b1_r, f1_r, b2_r, f2_r, pb_s, pb_r, pu_s, pu_r, pd_s, pd_r, r_s, r_r,
    c1_s, c1_r, c2_s, c2_r, out_s,
):
    s = lax.axis_index("section")
    z = lax.axis_index("dp")
    m = lax.axis_index("mp")
    x = lax.rem(m, 4)
    y = m // 4
    first = (1 - s) * x + s * y
    second = s * x + (1 - s) * y
    partner = (1 - s, z, m)

    barrier = pltpu.get_barrier_semaphore()

    @pl.loop(1, 16)
    def _(d):
        pl.semaphore_signal(barrier, inc=1, device_id=(s, lax.rem(z + d, 16), m), device_id_type=MESH)
        pl.semaphore_signal(barrier, inc=1, device_id=(s, z, lax.rem(m + d, 16)), device_id_type=MESH)

    pl.semaphore_signal(barrier, inc=1, device_id=partner, device_id_type=MESH)

    def spot(d, e):
        xx = lax.rem(x + (1 - s) * d + s * e, 4)
        yy = lax.rem(y + s * d + (1 - s) * e, 4)
        return yy * 4 + xx

    def remote(src, dst, ss, rs, to):
        return pltpu.make_async_remote_copy(
            src_ref=src, dst_ref=dst, send_sem=ss, recv_sem=rs, device_id=to, device_id_type=MESH
        )

    def lane(k):
        return pl.ds(pl.multiple_of(k * 128, 128), 128)

    small = [
        pltpu.make_async_copy(ffn_gain, fgain_v, loc.at[6]),
        pltpu.make_async_copy(sess, sess_v, loc.at[7]),
        pltpu.make_async_copy(hist, hist_v, loc.at[8]),
        pltpu.make_async_copy(gain, gain_v, loc.at[9]),
    ]
    locals_ = [
        pltpu.make_async_copy(w_uvqk.at[s, :, lane(m)], wa.at[z, s, :, lane(m)], loc.at[0]),
        pltpu.make_async_copy(w_out.at[s, :, lane(first)], wo.at[z, s, :, lane(first)], loc.at[1]),
        pltpu.make_async_copy(w_in, wi.at[pl.ds(0, 512), lane(16 * s + m)], loc.at[3]),
        pltpu.make_async_copy(events.at[0], ev, loc.at[2]),
        pltpu.make_async_copy(w_up, wu.at[s], loc.at[4]),
        pltpu.make_async_copy(w_down, wd.at[s], loc.at[5]),
    ]
    for c in locals_[:2] + small + locals_[2:]:
        c.start()

    pl.semaphore_wait(barrier, 31)
    locals_[0].wait()

    def z_copy(to_z):
        b = wa.at[z, s, :, lane(m)]
        return remote(b, b, z_s, z_r.at[z // 4], (s, to_z, m))

    def zo_copy(to_z):
        b = wo.at[z, s, :, lane(first)]
        return remote(b, b, zo_s, zo_r, (s, to_z, m))

    def arrived(ref, sem):
        remote(ref, ref, sem, sem, partner).wait_recv()

    def sent(ref, sem):
        remote(ref, ref, sem, sem, partner).wait_send()

    @pl.loop(1, 16)
    def _(d):
        z_copy(lax.rem(z + d, 16)).start()

    small[0].wait()
    wi[pl.ds(512, 16), lane(16 * s + m)] = jnp.broadcast_to(fgain_v[...], (16, 128))
    locals_[1].wait()
    locals_[2].wait()

    def win(mm, side):
        return wi.at[:, lane(16 * side + mm)]

    def half_win(mm, up):
        return wi.at[pl.ds(0, 256) if up > 0 else pl.ds(256, 272), lane(16 * s + mm)]

    def b1(up):
        b = win(m, s)
        return remote(b, b, b_s, b1_r.at[up], (s, z, spot(1 if up else 3, 0)))

    def b1_got(up):
        arrived(win(spot(3 if up else 1, 0), s), b1_r.at[up])

    def f1(up):
        b = half_win(spot(3 if up else 1, 0), up)
        return remote(b, b, f_s, f1_r, (s, z, spot(1 if up else 3, 0)))

    def f1_got():
        arrived(win(spot(2, 0), s), f1_r)

    def b2(d, up):
        b = win(spot(d, 0), s)
        return remote(b, b, b_s, b2_r.at[d, up], (s, z, spot(0, 1 if up else 3)))

    def b2_got(d, up):
        arrived(win(spot(d, 3 if up else 1), s), b2_r.at[d, up])

    def f2(d, up):
        b = half_win(spot(d, 3 if up else 1), up)
        return remote(b, b, f_s, f2_r.at[d], (s, z, spot(0, 1 if up else 3)))

    def f2_got(d):
        arrived(win(spot(d, 2), s), f2_r.at[d])

    def pb(d, e):
        b = win(spot(d, e), s)
        return remote(b, b, pb_s, pb_r, partner)

    for up in range(2):
        b1(up).start()
    for up in range(2):
        b2(0, up).start()

    pw = [
        remote(w_up, wu.at[s], pu_s, pu_r, partner),
        remote(w_down, wd.at[s], pd_s, pd_r, partner),
    ]
    pb(0, 0).start()
    for c in pw:
        c.start()

    @pl.loop(1, 16)
    def _(d):
        zo_copy(lax.rem(z + d, 16)).start()

    small[1].wait()
    small[2].wait()
    lens = jnp.broadcast_to(sess_v[...], (32, 32))
    at = lax.broadcasted_iota(jnp.int32, (32, 32), 0)
    of = lax.broadcasted_iota(jnp.int32, (32, 32), 1)
    ends = jnp.sum(jnp.where(of <= at, lens, 0).astype(F32), axis=1, keepdims=True)
    starts = jnp.sum(jnp.where(of < at, lens, 0).astype(F32), axis=1, keepdims=True)
    pos = lax.broadcasted_iota(jnp.int32, (32, 1024), 1).astype(F32)
    limit = jnp.minimum(ends, jnp.broadcast_to(hist_v[...], (32, 1)).astype(F32))
    inside = (pos >= starts) & (pos < limit)
    member[...] = jnp.where(inside, 1.0, 0.0).astype(BF)
    counts = jnp.maximum(limit - starts, 1.0)

    home, inner = z // 4, lax.rem(z, 4)
    step = 1 - 2 * ((5 - inner) // 4)
    groups = [home, lax.rem(home + step + 4, 4), lax.rem(home - step + 4, 4), lax.rem(home + 2, 4)]

    def block(g, mm):
        return wa.at[pl.ds(4 * g, 4), s, :, lane(mm)]

    def a1(i, d):
        b = block(groups[i], m)
        return remote(b, b, a1_s, a1_r.at[i], (s, z, spot(d, 0)))

    def a2(i, d, e):
        b = block(groups[i], spot(4 - d, 0))
        return remote(b, b, a2_s, a2_r.at[i], (s, z, spot(0, e)))

    def pa(i, side):
        b = wa.at[pl.ds(4 * groups[i], 4), side]
        return remote(b, b, pa_s, pa_r.at[i], partner)

    def oblock(ff):
        return wo.at[:, s, :, lane(ff)]

    def ao(d):
        b = oblock(first)
        return remote(b, b, ao_s, ao_r, (s, z, spot(d, 0)))

    def po(side):
        b = wo.at[:, side]
        return remote(b, b, po_s, po_r, partner)

    def from_z(i):
        g = groups[i]
        arrived(wa.at[pl.ds(4 * g, 3 if i == 0 else 4), s, :, lane(m)], z_r.at[g])
        for d in range(1, 4):
            a1(i, d).start()
        for e in range(1, 4):
            a2(i, 0, e).start()

    def from_first(i):
        arrived(wa.at[pl.ds(4 * groups[i], 4), s, :, pl.ds(0, 3 * 128)], a1_r.at[i])
        for d in range(1, 4):
            for e in range(1, 4):
                a2(i, d, e).start()

    def from_second(i):
        arrived(wa.at[pl.ds(4 * groups[i], 4), s, :, pl.ds(0, 12 * 128)], a2_r.at[i])
        pa(i, s).start()

    def pass_on(d):
        for up in range(2):
            b2_got(d, up)
            f2(d, up).start()
            pb(d, 3 if up else 1).start()

    def complete(d):
        f2_got(d)
        pb(d, 2).start()

    from_z(0)
    for up in range(2):
        b1_got(up)
        f1(up).start()
    from_z(1)
    from_first(0)
    from_z(2)
    from_first(1)
    from_z(3)
    from_first(2)
    from_first(3)
    for d in (3, 1):
        for up in range(2):
            b2(d, up).start()
        pb(d, 0).start()
    f1_got()
    for up in range(2):
        b2(2, up).start()
    pb(2, 0).start()
    arrived(wo.at[pl.ds(0, 15), s, :, lane(first)], zo_r)
    for d in range(1, 4):
        ao(d).start()
    from_second(0)
    from_second(1)
    from_second(2)
    locals_[3].wait()
    for i in range(2):
        pa(i, 1 - s).wait_recv()

    def tokens_of(lo, i, j):
        at_rows = pl.ds(lo, 256)
        return jnp.concatenate([ev[at_rows, lane(groups[i])], ev[at_rows, lane(groups[j])]], axis=1)

    def weights_of(c, i, j):
        cols = pl.ds(512 * c, 512)
        return jnp.concatenate(
            [wa[pl.ds(4 * groups[k], 4), :, :, cols].reshape(128, 512) for k in (i, j)], axis=0
        )

    for c in range(4):
        w = weights_of(c, 0, 1)
        for r in range(2):
            pre[pl.ds(256 * r, 256), pl.ds(512 * c, 512)] = dot(tokens_of(256 * r, 0, 1), w)

    from_second(3)
    pass_on(0)

    for i in range(2, 4):
        pa(i, 1 - s).wait_recv()

    small[3].wait()
    valid = jnp.broadcast_to(hist_v[...], (256, 1))

    def keep(r, parts):
        at_rows = pl.ds(r * 256, 256)
        row = r * 256 + lax.broadcasted_iota(jnp.int32, (256, 1), 0)
        gs[at_rows, :] = parts(0)
        vs[at_rows, :] = jnp.where(row < valid, parts(1), 0.0).astype(BF)
        qs[at_rows, :] = (parts(2) * (0.5 * 128 ** (-0.5))).astype(BF)
        ks[at_rows, :] = parts(3).astype(BF)

    def project(r):
        tokens = ev[pl.ds(r * 256, 256), :]
        keep(r, lambda c: silu(dot(tokens, wa[:, :, :, pl.ds(512 * c, 512)].reshape(512, 512))))

    def project_rest(r):
        tokens = tokens_of(256 * r, 2, 3)
        keep(
            r,
            lambda c: silu(
                pre[pl.ds(256 * r, 256), pl.ds(512 * c, 512)] + dot(tokens, weights_of(c, 2, 3))
            ),
        )

    diagonal = lax.broadcasted_iota(jnp.int32, (256, 256), 1) <= lax.broadcasted_iota(
        jnp.int32, (256, 256), 0
    )

    def attend(i, heads):
        lo = i * 256
        for h in heads:
            cols = pl.ds(h * 128, 128)
            q = qs[pl.ds(lo, 256), cols]

            def weigh(j):
                u = dot_nt(q, ks[pl.ds(256 * j, 256), cols])
                return u + u * jnp.tanh(u)

            acc = dot(
                jnp.where(diagonal, weigh(i), 0.0).astype(BF), vs[pl.ds(lo, 256), cols]
            )
            for j in range(i):
                acc += dot(weigh(j).astype(BF), vs[pl.ds(256 * j, 256), cols])
            att[pl.ds(lo, 256), cols] = acc

    def gate(i):
        at_rows = pl.ds(i * 256, 256)
        a = att[at_rows, :]
        inv = lax.rsqrt(jnp.mean(a * a, axis=1, keepdims=True) + EPSILON)
        gated[at_rows, :] = (a * inv * gain_v[...] * gs[at_rows, :]).astype(BF)

    def pool(nr, upto):
        mm = member[pl.ds(0, nr), pl.ds(0, upto)]
        pe = dot(mm, ev[pl.ds(0, upto), :])
        pg = dot(mm, gated[pl.ds(0, upto), :])
        hi = pg.astype(BF)
        lo = (pg - hi.astype(F32)).astype(BF)
        w = wo[...].reshape(512, 512)
        return pe + dot(hi, w) + dot(lo, w)

    for r in range(2):
        project_rest(r)
    arrived(wo.at[:, s, :, pl.ds(0, 3 * 128)], ao_r)
    po(s).start()
    pass_on(3)
    pass_on(1)
    for i in range(2):
        attend(i, range(4))
        gate(i)
    pass_on(2)
    complete(0)
    po(1 - s).wait_recv()
    early = (pool(16, 512) / counts[0:16])[0:8].astype(BF)
    slot = 4 * first + second
    rows[slot] = early

    def r_copy(to):
        return remote(rows.at[slot], rows.at[slot], r_s, r_r, (s, z, to))

    @pl.loop(1, 16)
    def _(d):
        r_copy(lax.rem(m + d, 16)).start()

    complete(3)
    complete(1)
    project(2)
    complete(2)
    project(3)

    arrived(rows.at[pl.ds(0, 15)], r_r)
    locals_[4].wait()
    locals_[5].wait()
    for c in pw:
        c.wait_recv()
    arrived(wi.at[:, pl.ds(pl.multiple_of((1 - s) * 2048, 128), 2048)], pb_r)

    xs = rows[...].astype(F32).reshape(128, 512).astype(BF)
    acc = jnp.zeros((128, 512), F32)
    sq = jnp.zeros((128, 1), F32)
    for c in range(8):
        cols = pl.ds(c * 512, 512)
        h = dot(xs, wi[pl.ds(0, 512), cols])
        hin[:, cols] = h
        g = wi[pl.ds(512, 16), cols].astype(F32)[0:1]
        acc += dot((h * g).astype(BF), wu[c // 4, pl.ds((c % 4) * 512, 512), :])
        sq += jnp.sum(h * h, axis=1, keepdims=True)
    up = acc * lax.rsqrt(sq * (1.0 / 4096) + EPSILON)
    hidden = jax.nn.gelu(up, approximate=True).astype(BF)

    def chunk(k):
        return pl.ds(k * 1024, 1024)

    def c1(k, d):
        to_first = lax.rem(first + d, 4)
        return remote(
            part.at[pl.ds(4 * to_first, 4), :, chunk(k)], recv.at[d - 1, :, :, chunk(k)],
            c1_s, c1_r.at[k], (s, z, spot(d, 0)),
        )

    def c2(k, e):
        return remote(
            relay.at[e - 1, :, chunk(k)], last.at[e - 1, :, chunk(k)],
            c2_s, c2_r.at[k], (s, z, spot(0, e)),
        )

    for k in range(4):
        p = dot(hidden, wd[k // 2, :, pl.ds((k % 2) * 1024, 1024)])
        part[:, :, chunk(k)] = p.reshape(16, 8, 1024).astype(BF)
        for d in range(1, 4):
            c1(k, d).start()

    def relay_chunk(k):
        arrived(recv.at[:, :, :, chunk(k)], c1_r.at[k])
        for e in (1, 2, 3, 0):
            gg = lax.rem(second + e, 4)
            t = part[4 * first + gg, :, chunk(k)].astype(F32)
            for d in range(1, 4):
                t += recv[d - 1, gg, :, chunk(k)].astype(F32)
            if e:
                relay[e - 1, :, chunk(k)] = t.astype(BF)
                c2(k, e).start()
            else:
                own[:, chunk(k)] = t + hin[pl.ds(pl.multiple_of(slot * 8, 8), 8), chunk(k)]

    def settle():
        sent(wa.at[pl.ds(0, 15), s, :, lane(m)], z_s)
        sent(wo.at[pl.ds(0, 15), s, :, lane(first)], zo_s)
        sent(rows.at[pl.ds(0, 15)], r_s)
        for c in pw:
            c.wait_send()
        sent(wa.at[pl.ds(0, 12), s, :, pl.ds(0, 512)], a1_s)
        sent(wa.at[:, s, :, pl.ds(0, 12 * 128)], a2_s)
        sent(wa.at[:, s], pa_s)
        sent(wo.at[:, s, :, pl.ds(0, 3 * 128)], ao_s)
        po(s).wait_send()
        sent(wi.at[:, pl.ds(0, 10 * 128)], b_s)
        sent(wi.at[:, pl.ds(0, 5 * 128)], f_s)
        sent(wi.at[:, pl.ds(0, 16 * 128)], pb_s)

    attend(2, (0, 1))
    attend(2, (2, 3))
    gate(2)
    relay_chunk(0)
    attend(3, (0, 1))
    relay_chunk(1)
    attend(3, (2, 3))
    relay_chunk(2)
    gate(3)
    pooled_v[...] = (pool(32, 1024) / counts).astype(BF)
    outs = [pltpu.make_async_copy(pooled_v, pooled_out, out_s.at[0])]
    outs[0].start()
    relay_chunk(3)
    settle()
    for k in range(4):
        t = own[:, chunk(k)]
        arrived(last.at[:, :, chunk(k)], c2_r.at[k])
        for e in range(1, 4):
            t += last[e - 1, :, chunk(k)].astype(F32)
        cross_v[:, chunk(k)] = t.astype(BF)
        outs.append(
            pltpu.make_async_copy(cross_v.at[:, chunk(k)], cross_out.at[:, chunk(k)], out_s.at[k + 1])
        )
        outs[-1].start()
    sent(recv, c1_s)
    sent(relay, c2_s)
    for c in outs:
        c.wait()


def hand_on(pooled, cross, pooled_out, cross_out):
    pooled_out[...] = pooled[...]
    cross_out[...] = cross[...]


def per_device(events, hist_len, sess_len, w_uvqk, w_out, attn_gain, w_in, ffn_gain, w_up, w_down):
    anywhere = pl.BlockSpec(memory_space=pl.ANY)
    vm = pltpu.VMEM
    outs = (jax.ShapeDtypeStruct((32, 512), BF), jax.ShapeDtypeStruct((8, 4096), BF))
    both = pl.pallas_call(
        kernel,
        out_shape=outs,
        in_specs=[anywhere] * 10,
        out_specs=(anywhere, anywhere),
        scratch_shapes=[
            vm((1, 1), jnp.int32),
            vm((1, 32), jnp.int32),
            vm((1, 512), F32),
            vm((1, 128), BF),
            vm((32, 512), BF),
            vm((8, 4096), BF),
            vm((1024, 512), BF),
            vm((16, 2, 16, 2048), BF),
            vm((16, 2, 16, 512), BF),
            vm((528, 4096), BF),
            vm((2, 2048, 512), BF),
            vm((2, 512, 2048), BF),
            vm((1024, 512), BF),
            vm((1024, 512), BF),
            vm((1024, 512), BF),
            vm((1024, 512), F32),
            vm((1024, 512), F32),
            vm((1024, 512), BF),
            vm((32, 1024), BF),
            vm((16, 8, 512), BF),
            vm((128, 4096), F32),
            vm((16, 8, 4096), BF),
            vm((3, 4, 8, 4096), BF),
            vm((3, 8, 4096), BF),
            vm((3, 8, 4096), BF),
            vm((8, 4096), F32),
            vm((512, 2048), F32),
            DMA((10,)),
            DMA, DMA((4,)), DMA, DMA,
            DMA, DMA((4,)), DMA, DMA,
            DMA, DMA((4,)),
            DMA, DMA((4,)), DMA, DMA,
            DMA, DMA, DMA((2,)), DMA, DMA((4, 2)), DMA((4,)),
            DMA, DMA,
            DMA, DMA, DMA, DMA,
            DMA, DMA,
            DMA, DMA((4,)), DMA, DMA((4,)),
            DMA((5,)),
        ],
        compiler_params=pltpu.CompilerParams(
            collective_id=0, has_side_effects=True, vmem_limit_bytes=60 << 20
        ),
        name="encode_and_mix",
    )(
        events, hist_len.reshape(1, 1), sess_len, w_uvqk.reshape(2, 16, 2048), w_out.reshape(2, 16, 512),
        attn_gain.reshape(1, 512), w_in, ffn_gain, w_up, w_down,
    )
    return pl.pallas_call(hand_on, out_shape=outs, name="hand_on")(*both)


def solution(mesh):
    return jax.shard_map(
        per_device,
        mesh=mesh,
        in_specs=(
            P(("section", "dp", "mp"), None, None),
            P(("section", "dp", "mp")),
            P(("section", "dp", "mp"), None),
            P("dp", None),
            P("dp", None),
            P(),
            P(None, ("section", "mp")),
            P(None, ("section", "mp")),
            P("section", "mp"),
            P("mp", "section"),
        ),
        out_specs=(P(("section", "dp", "mp"), None), P(("section", "dp", "mp"), None)),
        check_vma=False,
    )
```

time: 84.3 us -> 66.6 us (0.79)
  the two profiles are of different devices: /device:TPU:1 before, /device:TPU:4 now
where the time goes in v2:
time: 66.6 us; the launch traced here: 66.5 us
  Pallas kernels  65.2 us (98%)
  between operations  1.29 us (2%)
    pallas_call x1, Pallas kernels, per_device(): pl.pallas_call(kernel, out_shape=outs, in_specs=[anywhere] * 10, out_spec...  63.7 us
    pallas_call x1, Pallas kernels, per_device(): return pl.pallas_call(hand_on, out_shape=outs, name='hand_on')(*both)  1.5 us

profile of v2, /device:TPU:4, one launch (start us, length us, event | category | flops | bytes accessed | tf_op | source)
XLA Modules:
  0.0 66.5 jit_solution(7932202900429021710)
XLA Ops:
  1.3 63.7 %encode_and_mix.1 = (bf16[32,512]{1,0:T(8,128)(2,1)}, bf16[8,4096]{1,0:T(8,128)(2,1)}) custom-call(bf16[1,1024,512]{2,1,0:T(8,128)(2,1)} %events.1, s32[1,1]{1,0:T(1,128)} %bitcast.4.hist, s32[1,32]{1,0:T(1,128)} %sess.1, bf16[2,16,2048]{2,1,0:T(8,128)(2,1)} %bitcast.5, bf16[2,16,512]{2,1,0:T(8,128)(2,1)} %bitcast.6, f32[1,512]{1,0:T(1,128)} %bitcast.7, ...), custom_call_target="tpu_custom_call" | custom-call | tf_op jit(solution)/shard_map/encode_and_mix/pallas_call | solution.py:485
  65.0 1.5 %hand_on.1 = (bf16[32,512]{1,0:T(8,128)(2,1)}, bf16[8,4096]{1,0:T(8,128)(2,1)}) custom-call(bf16[32,512]{1,0:T(8,128)(2,1)} %get-tuple-element.4.pooled, bf16[8,4096]{1,0:T(8,128)(2,1)} %get-tuple-element.5.cross), custom_call_target="tpu_custom_call" | custom-call | tf_op jit(solution)/shard_map/hand_on/pallas_call | solution.py:538

commit v3 on v2

--- a/solution.py
+++ b/solution.py
@@ -20,17 +20,18 @@
     return lax.dot_general(a, b, (((1,), (1,)), ((), ())), preferred_element_type=F32)
 
 
-def silu(v):
-    half = 0.5 * v
-    return half + half * jnp.tanh(half)
+def silu(v, scale=None):
+    half = (0.5 * v).astype(BF)
+    first = half if scale is None else ((0.5 * scale) * v).astype(BF)
+    return first + first * jnp.tanh(half)
 
 
 def kernel(
     events, hist, sess, w_uvqk, w_out, gain, w_in, ffn_gain, w_up, w_down,
     pooled_out, cross_out,
-    hist_v, sess_v, gain_v, fgain_v, pooled_v, cross_v,
+    hist_s, sess_v, gain_v, fgain_v, pooled_v, cross_v,
     ev, wa, wo, wi, wu, wd, qs, ks, vs, gs, att, gated, member, rows, hin, part, recv, relay, last, own,
-    pre, loc, z_s, z_r, zo_s, zo_r, a1_s, a1_r, ao_s, ao_r, a2_s, a2_r, pa_s, pa_r, po_s, po_r,
+    pre, pooled_ev, loc, z_s, z_r, zo_s, zo_r, a1_s, a1_r, ao_s, ao_r, a2_s, a2_r, pa_s, pa_r, po_s, po_r,
     b_s, f_s, b1_r, f1_r, b2_r, f2_r, pb_s, pb_r, pu_s, pu_r, pd_s, pd_r, r_s, r_r,
     c1_s, c1_r, c2_s, c2_r, out_s,
 ):
@@ -68,7 +69,7 @@
     small = [
         pltpu.make_async_copy(ffn_gain, fgain_v, loc.at[6]),
         pltpu.make_async_copy(sess, sess_v, loc.at[7]),
-        pltpu.make_async_copy(hist, hist_v, loc.at[8]),
+        pltpu.make_async_copy(hist, hist_s, loc.at[8]),
         pltpu.make_async_copy(gain, gain_v, loc.at[9]),
     ]
     locals_ = [
@@ -99,12 +100,13 @@
     def sent(ref, sem):
         remote(ref, ref, sem, sem, partner).wait_send()
 
+    small[0].wait()
+    wi[pl.ds(512, 16), lane(16 * s + m)] = jnp.broadcast_to(fgain_v[...], (16, 128))
+
     @pl.loop(1, 16)
     def _(d):
         z_copy(lax.rem(z + d, 16)).start()
 
-    small[0].wait()
-    wi[pl.ds(512, 16), lane(16 * s + m)] = jnp.broadcast_to(fgain_v[...], (16, 128))
     locals_[1].wait()
     locals_[2].wait()
 
@@ -171,10 +173,12 @@
     ends = jnp.sum(jnp.where(of <= at, lens, 0).astype(F32), axis=1, keepdims=True)
     starts = jnp.sum(jnp.where(of < at, lens, 0).astype(F32), axis=1, keepdims=True)
     pos = lax.broadcasted_iota(jnp.int32, (32, 1024), 1).astype(F32)
-    limit = jnp.minimum(ends, jnp.broadcast_to(hist_v[...], (32, 1)).astype(F32))
+    limit = jnp.minimum(ends, hist_s[0].astype(F32))
     inside = (pos >= starts) & (pos < limit)
     member[...] = jnp.where(inside, 1.0, 0.0).astype(BF)
     counts = jnp.maximum(limit - starts, 1.0)
+    locals_[3].wait()
+    pooled_ev[...] = dot(member[...], ev[...])
 
     home, inner = z // 4, lax.rem(z, 4)
     step = 1 - 2 * ((5 - inner) // 4)
@@ -209,15 +213,15 @@
     def from_z(i):
         g = groups[i]
         arrived(wa.at[pl.ds(4 * g, 3 if i == 0 else 4), s, :, lane(m)], z_r.at[g])
-        for d in range(1, 4):
+        for d in (2, 1, 3):
             a1(i, d).start()
-        for e in range(1, 4):
+        for e in (2, 1, 3):
             a2(i, 0, e).start()
 
     def from_first(i):
         arrived(wa.at[pl.ds(4 * groups[i], 4), s, :, pl.ds(0, 3 * 128)], a1_r.at[i])
-        for d in range(1, 4):
-            for e in range(1, 4):
+        for e in (2, 1, 3):
+            for d in range(1, 4):
                 a2(i, d, e).start()
 
     def from_second(i):
@@ -235,31 +239,33 @@
         pb(d, 2).start()
 
     from_z(0)
+    from_z(1)
     for up in range(2):
         b1_got(up)
         f1(up).start()
-    from_z(1)
+    pb(3, 0).start()
+    pb(1, 0).start()
+    from_z(2)
+    from_z(3)
     from_first(0)
-    from_z(2)
     from_first(1)
-    from_z(3)
     from_first(2)
     from_first(3)
     for d in (3, 1):
         for up in range(2):
             b2(d, up).start()
-        pb(d, 0).start()
     f1_got()
     for up in range(2):
         b2(2, up).start()
-    pb(2, 0).start()
+    pass_on(0)
     arrived(wo.at[pl.ds(0, 15), s, :, lane(first)], zo_r)
     for d in range(1, 4):
         ao(d).start()
     from_second(0)
     from_second(1)
     from_second(2)
-    locals_[3].wait()
+    from_second(3)
+    pb(2, 0).start()
     for i in range(2):
         pa(i, 1 - s).wait_recv()
 
@@ -278,34 +284,31 @@
         for r in range(2):
             pre[pl.ds(256 * r, 256), pl.ds(512 * c, 512)] = dot(tokens_of(256 * r, 0, 1), w)
 
-    from_second(3)
-    pass_on(0)
-
     for i in range(2, 4):
         pa(i, 1 - s).wait_recv()
 
     small[3].wait()
-    valid = jnp.broadcast_to(hist_v[...], (256, 1))
 
     def keep(r, parts):
         at_rows = pl.ds(r * 256, 256)
-        row = r * 256 + lax.broadcasted_iota(jnp.int32, (256, 1), 0)
-        gs[at_rows, :] = parts(0)
-        vs[at_rows, :] = jnp.where(row < valid, parts(1), 0.0).astype(BF)
-        qs[at_rows, :] = (parts(2) * (0.5 * 128 ** (-0.5))).astype(BF)
-        ks[at_rows, :] = parts(3).astype(BF)
+        gs[at_rows, :] = silu(parts(0))
+        values = silu(parts(1))
+        if r:
+            row = r * 256 + lax.broadcasted_iota(jnp.int32, (256, 1), 0)
+            values *= jnp.where(row < hist_s[0], 1.0, 0.0).astype(BF)
+        vs[at_rows, :] = values
+        qs[at_rows, :] = silu(parts(2), 128 ** (-0.5) * 0.5)
+        ks[at_rows, :] = silu(parts(3))
 
     def project(r):
         tokens = ev[pl.ds(r * 256, 256), :]
-        keep(r, lambda c: silu(dot(tokens, wa[:, :, :, pl.ds(512 * c, 512)].reshape(512, 512))))
+        keep(r, lambda c: dot(tokens, wa[:, :, :, pl.ds(512 * c, 512)].reshape(512, 512)))
 
     def project_rest(r):
         tokens = tokens_of(256 * r, 2, 3)
         keep(
             r,
-            lambda c: silu(
-                pre[pl.ds(256 * r, 256), pl.ds(512 * c, 512)] + dot(tokens, weights_of(c, 2, 3))
-            ),
+            lambda c: pre[pl.ds(256 * r, 256), pl.ds(512 * c, 512)] + dot(tokens, weights_of(c, 2, 3)),
         )
 
     diagonal = lax.broadcasted_iota(jnp.int32, (256, 256), 1) <= lax.broadcasted_iota(
@@ -320,29 +323,27 @@
 
             def weigh(j):
                 u = dot_nt(q, ks[pl.ds(256 * j, 256), cols])
+                u = (jnp.where(diagonal, u, 0.0) if j == i else u).astype(BF)
                 return u + u * jnp.tanh(u)
 
-            acc = dot(
-                jnp.where(diagonal, weigh(i), 0.0).astype(BF), vs[pl.ds(lo, 256), cols]
-            )
+            acc = dot(weigh(i), vs[pl.ds(lo, 256), cols])
             for j in range(i):
-                acc += dot(weigh(j).astype(BF), vs[pl.ds(256 * j, 256), cols])
+                acc += dot(weigh(j), vs[pl.ds(256 * j, 256), cols])
             att[pl.ds(lo, 256), cols] = acc
 
     def gate(i):
         at_rows = pl.ds(i * 256, 256)
         a = att[at_rows, :]
         inv = lax.rsqrt(jnp.mean(a * a, axis=1, keepdims=True) + EPSILON)
-        gated[at_rows, :] = (a * inv * gain_v[...] * gs[at_rows, :]).astype(BF)
+        gated[at_rows, :] = (a * inv * gain_v[...] * gs[at_rows, :].astype(F32)).astype(BF)
 
     def pool(nr, upto):
         mm = member[pl.ds(0, nr), pl.ds(0, upto)]
-        pe = dot(mm, ev[pl.ds(0, upto), :])
         pg = dot(mm, gated[pl.ds(0, upto), :])
         hi = pg.astype(BF)
         lo = (pg - hi.astype(F32)).astype(BF)
-        w = wo[...].reshape(512, 512)
-        return pe + dot(hi, w) + dot(lo, w)
+        both = dot(jnp.concatenate([hi, lo], axis=0), wo[...].reshape(512, 512))
+        return pooled_ev[pl.ds(0, nr), :] + both[0:nr] + both[nr : 2 * nr]
 
     for r in range(2):
         project_rest(r)
@@ -367,6 +368,7 @@
     def _(d):
         r_copy(lax.rem(m + d, 16)).start()
 
+
     complete(3)
     complete(1)
     project(2)
@@ -383,12 +385,12 @@
     xs = rows[...].astype(F32).reshape(128, 512).astype(BF)
     acc = jnp.zeros((128, 512), F32)
     sq = jnp.zeros((128, 1), F32)
-    for c in range(8):
-        cols = pl.ds(c * 512, 512)
+    for c in range(2):
+        cols = pl.ds(c * 2048, 2048)
         h = dot(xs, wi[pl.ds(0, 512), cols])
         hin[:, cols] = h
         g = wi[pl.ds(512, 16), cols].astype(F32)[0:1]
-        acc += dot((h * g).astype(BF), wu[c // 4, pl.ds((c % 4) * 512, 512), :])
+        acc += dot((h * g).astype(BF), wu[c])
         sq += jnp.sum(h * h, axis=1, keepdims=True)
     up = acc * lax.rsqrt(sq * (1.0 / 4096) + EPSILON)
     hidden = jax.nn.gelu(up, approximate=True).astype(BF)
@@ -412,21 +414,29 @@
     for k in range(4):
         p = dot(hidden, wd[k // 2, :, pl.ds((k % 2) * 1024, 1024)])
         part[:, :, chunk(k)] = p.reshape(16, 8, 1024).astype(BF)
-        for d in range(1, 4):
-            c1(k, d).start()
+
+        @pl.loop(0, 3)
+        def _(i):
+            c1(k, 1 + lax.rem(i + 1, 3)).start()
+
 
     def relay_chunk(k):
         arrived(recv.at[:, :, :, chunk(k)], c1_r.at[k])
-        for e in (1, 2, 3, 0):
+        def total(e):
             gg = lax.rem(second + e, 4)
             t = part[4 * first + gg, :, chunk(k)].astype(F32)
             for d in range(1, 4):
                 t += recv[d - 1, gg, :, chunk(k)].astype(F32)
-            if e:
-                relay[e - 1, :, chunk(k)] = t.astype(BF)
-                c2(k, e).start()
-            else:
-                own[:, chunk(k)] = t + hin[pl.ds(pl.multiple_of(slot * 8, 8), 8), chunk(k)]
+            return t
+
+        for e in range(1, 4):
+            relay[e - 1, :, chunk(k)] = total(e).astype(BF)
+
+        @pl.loop(0, 3)
+        def _(i):
+            c2(k, 1 + lax.rem(i + 1, 3)).start()
+
+        own[:, chunk(k)] = total(0) + hin[pl.ds(pl.multiple_of(slot * 8, 8), 8), chunk(k)]
 
     def settle():
         sent(wa.at[pl.ds(0, 15), s, :, lane(m)], z_s)
@@ -453,9 +463,9 @@
     relay_chunk(2)
     gate(3)
     pooled_v[...] = (pool(32, 1024) / counts).astype(BF)
-    outs = [pltpu.make_async_copy(pooled_v, pooled_out, out_s.at[0])]
-    outs[0].start()
     relay_chunk(3)
+    pooled_copy = pltpu.make_async_copy(pooled_v, pooled_out, out_s.at[0])
+    pooled_copy.start()
     settle()
     for k in range(4):
         t = own[:, chunk(k)]
@@ -463,14 +473,20 @@
         for e in range(1, 4):
             t += last[e - 1, :, chunk(k)].astype(F32)
         cross_v[:, chunk(k)] = t.astype(BF)
-        outs.append(
-            pltpu.make_async_copy(cross_v.at[:, chunk(k)], cross_out.at[:, chunk(k)], out_s.at[k + 1])
-        )
-        outs[-1].start()
+
+    def cross_copy(k):
+        cols = pl.ds(pl.multiple_of(k * 1024, 1024), 1024)
+        return pltpu.make_async_copy(cross_v.at[:, cols], cross_out.at[:, cols], out_s.at[k + 1])
+
+    @pl.loop(0, 4)
+    def _(k):
+        cross_copy(k).start()
+
     sent(recv, c1_s)
     sent(relay, c2_s)
-    for c in outs:
-        c.wait()
+    pooled_copy.wait()
+    for k in range(4):
+        cross_copy(k).wait()
 
 
 def hand_on(pooled, cross, pooled_out, cross_out):
@@ -488,7 +504,7 @@
         in_specs=[anywhere] * 10,
         out_specs=(anywhere, anywhere),
         scratch_shapes=[
-            vm((1, 1), jnp.int32),
+            pltpu.SMEM((1,), jnp.int32),
             vm((1, 32), jnp.int32),
             vm((1, 512), F32),
             vm((1, 128), BF),
@@ -503,7 +519,7 @@
             vm((1024, 512), BF),
             vm((1024, 512), BF),
             vm((1024, 512), BF),
-            vm((1024, 512), F32),
+            vm((1024, 512), BF),
             vm((1024, 512), F32),
             vm((1024, 512), BF),
             vm((32, 1024), BF),
@@ -515,6 +531,7 @@
             vm((3, 8, 4096), BF),
             vm((8, 4096), F32),
             vm((512, 2048), F32),
+            vm((32, 512), F32),
             DMA((10,)),
             DMA, DMA((4,)), DMA, DMA,
             DMA, DMA((4,)), DMA, DMA,
@@ -532,7 +549,7 @@
         ),
         name="encode_and_mix",
     )(
-        events, hist_len.reshape(1, 1), sess_len, w_uvqk.reshape(2, 16, 2048), w_out.reshape(2, 16, 512),
+        events, hist_len, sess_len, w_uvqk.reshape(2, 16, 2048), w_out.reshape(2, 16, 512),
         attn_gain.reshape(1, 512), w_in, ffn_gain, w_up, w_down,
     )
     return pl.pallas_call(hand_on, out_shape=outs, name="hand_on")(*both)

time: 66.6 us -> 64.3 us (0.965)
  the two profiles are of different devices: /device:TPU:4 before, /device:TPU:8 now
where the time goes in v3:
time: 64.3 us; the launch traced here: 64.1 us
  Pallas kernels  62.8 us (98%)
  between operations  1.29 us (2%)
    pallas_call x1, Pallas kernels, per_device(): pl.pallas_call(kernel, out_shape=outs, in_specs=[anywhere] * 10, out_spec...  61.3 us
    pallas_call x1, Pallas kernels, per_device(): return pl.pallas_call(hand_on, out_shape=outs, name='hand_on')(*both)  1.5 us

profile of v3, /device:TPU:8, one launch (start us, length us, event | category | flops | bytes accessed | tf_op | source)
XLA Modules:
  0.0 64.1 jit_solution(2698575733812093890)
XLA Ops:
  1.3 61.3 %encode_and_mix.1 = (bf16[32,512]{1,0:T(8,128)(2,1)}, bf16[8,4096]{1,0:T(8,128)(2,1)}) custom-call(bf16[1,1024,512]{2,1,0:T(8,128)(2,1)} %events.1, s32[1]{0:T(128)S(6)} %copy.12.hist, s32[1,32]{1,0:T(1,128)} %sess.1, bf16[2,16,2048]{2,1,0:T(8,128)(2,1)} %bitcast.3, bf16[2,16,512]{2,1,0:T(8,128)(2,1)} %bitcast.4, f32[1,512]{1,0:T(1,128)} %bitcast.5, ...), custom_call_target="tpu_custom_call" | custom-call | tf_op jit(solution)/shard_map/encode_and_mix/pallas_call | solution.py:501
  62.6 1.5 %hand_on.1 = (bf16[32,512]{1,0:T(8,128)(2,1)}, bf16[8,4096]{1,0:T(8,128)(2,1)}) custom-call(bf16[32,512]{1,0:T(8,128)(2,1)} %get-tuple-element.4.pooled, bf16[8,4096]{1,0:T(8,128)(2,1)} %get-tuple-element.5.cross), custom_call_target="tpu_custom_call" | custom-call | tf_op jit(solution)/shard_map/hand_on/pallas_call | solution.py:555

commit v4 on v3

--- a/solution.py
+++ b/solution.py
@@ -350,12 +350,13 @@
     arrived(wo.at[:, s, :, pl.ds(0, 3 * 128)], ao_r)
     po(s).start()
     pass_on(3)
+    attend(0, range(4))
+    gate(0)
     pass_on(1)
-    for i in range(2):
-        attend(i, range(4))
-        gate(i)
     pass_on(2)
     complete(0)
+    attend(1, range(4))
+    gate(1)
     po(1 - s).wait_recv()
     early = (pool(16, 512) / counts[0:16])[0:8].astype(BF)
     slot = 4 * first + second

time: 64.3 us -> 65.4 us (1.017)
  Pallas kernels: 62.8 us -> 64 us
    pallas_call x1, Pallas kernels: 61.3 us -> 62.5 us  [per_device(): pl.pallas_call(kernel, out_shape=outs, in_specs=[anywhere] * 10, out_spec...]
where the time goes in v4:
time: 65.4 us; the launch traced here: 65.2 us
  Pallas kernels  64 us (98%)
  between operations  1.29 us (2%)
    pallas_call x1, Pallas kernels, per_device(): pl.pallas_call(kernel, out_shape=outs, in_specs=[anywhere] * 10, out_spec...  62.5 us
    pallas_call x1, Pallas kernels, per_device(): return pl.pallas_call(hand_on, out_shape=outs, name='hand_on')(*both)  1.5 us

profile of v4, /device:TPU:8, one launch (start us, length us, event | category | flops | bytes accessed | tf_op | source)
XLA Modules:
  0.0 65.2 jit_solution(575012764262059936)
XLA Ops:
  1.3 62.5 %encode_and_mix.1 = (bf16[32,512]{1,0:T(8,128)(2,1)}, bf16[8,4096]{1,0:T(8,128)(2,1)}) custom-call(bf16[1,1024,512]{2,1,0:T(8,128)(2,1)} %events.1, s32[1]{0:T(128)S(6)} %copy.12.hist, s32[1,32]{1,0:T(1,128)} %sess.1, bf16[2,16,2048]{2,1,0:T(8,128)(2,1)} %bitcast.3, bf16[2,16,512]{2,1,0:T(8,128)(2,1)} %bitcast.4, f32[1,512]{1,0:T(1,128)} %bitcast.5, ...), custom_call_target="tpu_custom_call" | custom-call | tf_op jit(solution)/shard_map/encode_and_mix/pallas_call | solution.py:502
  63.7 1.5 %hand_on.1 = (bf16[32,512]{1,0:T(8,128)(2,1)}, bf16[8,4096]{1,0:T(8,128)(2,1)}) custom-call(bf16[32,512]{1,0:T(8,128)(2,1)} %get-tuple-element.4.pooled, bf16[8,4096]{1,0:T(8,128)(2,1)} %get-tuple-element.5.cross), custom_call_target="tpu_custom_call" | custom-call | tf_op jit(solution)/shard_map/hand_on/pallas_call | solution.py:556
